TPU v7x, 512 devices: a whole 4x8x8 slice. The times are simulated.
512 devices in a mesh: lon: 32 (over z_lo, y), lat: 16 (over z_hi, x, core).
Axes of the slice: x: 4, y: 8, z: 8 (z_hi: 2, z_lo: 4; z = z_hi * 4 + z_lo), core: 2. Of those that a mesh axis runs over, the one named last changes fastest.
Arguments:
- wind_u: float32 [720, 1440, 16], P('lat', 'lon'), may hold values from -6 to 6
- wind_v: float32 [720, 1440, 16], P('lat', 'lon'), may hold values from -6 to 6
- vorticity: float32 [720, 1440, 16], P('lat', 'lon'), may hold values from -6 to 6
- sample_level: int32 [16], replicated, may hold values from 0 to 1, as said below
- slot_wavenumber: int32 [736], P('lon'), may hold values from -1 to 719, as said below
- legendre_p: bfloat16 [720, 529920], P('lat', 'lon'), may hold values from -5 to 5
- legendre_h: bfloat16 [720, 529920], P('lat', 'lon'), may hold values from -5 to 5
Outputs:
- spectra: float32 [2, 529920], P(None, ('lon', 'lat'))
Inputs may be any that keep to these rules, and one draw needn't show every extreme that they name: `sample_level`: each level is named by exactly 8 samples. `slot_wavenumber`: each wavenumber from 0 to 719 stands in exactly one slot; the remaining slots hold -1.
All inputs are finite; a program needn't handle non-finite values.
Results may differ from a plain program's by a relative error of at most 0.0014.
Values sent between devices are 32-bit elements; how exact they have to be, the bound alone decides.
A program may use at most 128 MiB of HBM per device.

v0:
```python
import math
import jax
import jax.numpy as jnp
from jax import lax
from jax.sharding import PartitionSpec as P

NLON = 1440
NLAT = 720
MAXM = 720
LEV = 2
DAYS = 8
S = 16


def remove_means(field, onehot):
    means = jnp.einsum("jis,sl->jil", field, onehot, precision=lax.Precision.HIGHEST) / DAYS
    return field - jnp.einsum("jil,sl->jis", means, onehot, precision=lax.Precision.HIGHEST)


def fourier_table(waves, count):
    longitude = jnp.arange(count, dtype=jnp.int32)
    present = waves >= 0
    clipped = jnp.maximum(waves, 0)
    residue = longitude[:, None] * clipped[None, :] % NLON
    angle = residue.astype(jnp.float32) * (2.0 * math.pi / NLON)
    weight = present.astype(jnp.float32)[None, :] / NLON
    return jnp.stack([jnp.cos(angle) * weight, jnp.sin(angle) * weight], axis=2)


def body(wind_u, wind_v, vorticity, sample_level, slot_wavenumber, legendre_p, legendre_h):
    band_rows = wind_u.shape[0]
    lat_count = lax.axis_size("lat")
    onehot = (sample_level[:, None] == jnp.arange(LEV, dtype=jnp.int32)[None, :]).astype(
        jnp.float32
    )
    eddy_u = remove_means(wind_u, onehot)
    eddy_v = remove_means(wind_v, onehot)
    eddy_z = remove_means(vorticity, onehot)
    row_index = lax.axis_index("lat") * band_rows + jnp.arange(band_rows, dtype=jnp.int32)
    latitude = (row_index.astype(jnp.float32) + 0.5) * (math.pi / NLAT) - 0.5 * math.pi
    cosine = jnp.cos(latitude)[:, None, None]
    fluxes = jnp.concatenate([eddy_u * eddy_z * cosine, eddy_v * eddy_z * cosine], axis=2)
    owned_count = slot_wavenumber.shape[0]
    piece = lax.all_gather(fluxes, "lon", axis=1, tiled=True)
    table = fourier_table(slot_wavenumber, piece.shape[1])
    coeffs = jnp.einsum("jic,iqt->jqtc", piece, table, precision=lax.Precision.HIGHEST)
    present = slot_wavenumber >= 0
    clipped = jnp.maximum(slot_wavenumber, 0)
    scale = (clipped.astype(jnp.float32) / MAXM)[None, :, None]
    cos_u = coeffs[:, :, 0, :S]
    sin_u = coeffs[:, :, 1, :S]
    cos_v = coeffs[:, :, 0, S:]
    sin_v = coeffs[:, :, 1, S:]
    right_p = jnp.concatenate([scale * sin_u, scale * cos_u], axis=2).astype(jnp.bfloat16)
    right_h = jnp.concatenate([-cos_v, sin_v], axis=2).astype(jnp.bfloat16)
    table_p = legendre_p.reshape(band_rows, owned_count, MAXM)
    table_h = legendre_h.reshape(band_rows, owned_count, MAXM)
    partial_sum = jnp.einsum("jqn,jqc->qnc", table_p, right_p, preferred_element_type=jnp.float32)
    partial_sum = partial_sum + jnp.einsum(
        "jqn,jqc->qnc", table_h, right_h, preferred_element_type=jnp.float32
    )
    degree = jnp.arange(MAXM, dtype=jnp.int32)
    keep = ((degree[None, :] >= clipped[:, None]) & present[:, None]).astype(jnp.float32)
    flat_terms = (partial_sum * keep[:, :, None]).reshape(owned_count * MAXM, 2 * S)
    share = flat_terms.shape[0] // lat_count
    summed = lax.psum(flat_terms, "lat")
    mine = lax.dynamic_slice_in_dim(summed, lax.axis_index("lat") * share, share, 0)
    power = mine[:, :S] ** 2 + mine[:, S:] ** 2
    spectra = jnp.dot(power, onehot, precision=lax.Precision.HIGHEST) / DAYS
    return spectra.T


def solution(mesh):
    placed = (
        P("lat", "lon", None),
        P("lat", "lon", None),
        P("lat", "lon", None),
        P(),
        P("lon"),
        P("lat", "lon"),
        P("lat", "lon"),
    )
    return jax.shard_map(
        body, mesh=mesh, in_specs=placed, out_specs=P(None, ("lon", "lat")), check_vma=False
    )
```

profile of v0, /device:TPU:1, one launch (start us, length us, event | category | flops | bytes accessed | tf_op | source)
XLA Modules:
  0.0 525.2 jit_solution(9790209907816465756)
XLA Ops:
  6.5 0.0 copy-start.2
  6.5 0.0 copy-start
  6.5 0.0 copy-start.1
  6.5 0.0 all-gather.2.cloned.1.call-start
  6.6 1.3 fusion.16
  7.9 1.4 convolution_subtract_fusion.1
  9.3 1.2 fusion.15
  10.5 1.2 fusion.17
  11.8 0.0 copy-done
  11.8 1.1 fusion.13
  12.9 0.0 copy-done.2
  12.9 0.0 copy-done.1
  12.9 0.4 fusion.14
  13.3 0.1 pad_maximum_fusion
  13.4 1.7 copy.19
  15.1 0.0 all-gather.2.cloned.1.call-update
  15.1 0.2 all-reduce.2.cloned.1.call-start
  15.3 4.0 reshape.180
  19.3 0.0 copy-start.3
  19.3 4.0 reshape.179
  23.4 0.0 copy-done.3
  23.4 0.1 fusion.37
  23.5 1.4 cosine_multiply_fusion
  24.9 262.6 %all-gather.2.cloned.1.call-done = f32[45,1440,32]{0,2,1:T(8,128)} async-done(((f32[45,45,32]{0,2,1:T(8,128)}), f32[45,1440,32]{0,2,1:T(8,128)}) %all-gather.2.cloned.1.call-update) | async-done | bytes 8294416 | tf_op jit(solution)/shard_map/all_gather | solution.py:44
  287.4 17.4 %copy.20 = f32[45,1440,32]{1,0,2:T(8,128)} copy(f32[45,1440,32]{0,2,1:T(8,128)} %all-gather.2.cloned.1.call-done) | data formatting | bytes 16588800 | tf_op jit(solution)/shard_map/all_gather | solution.py:44
  304.8 18.9 %fusion.8 = f32[45,23,2,32]{0,1,3,2:T(8,128)S(1)} fusion(f32[45,1440,32]{1,0,2:T(8,128)} %copy.20, f32[1440,23,1]{0,1,2:T(8,128)} %get-tuple-element.8, f32[1440,23,1]{0,1,2:T(8,128)S(1)} %get-tuple-element.7), kind=kOutput, calls=%fused_computation.8 | convolution fusion | flops 1144693504 | bytes 8824320 | tf_op jit(solution)/shard_map/jic,iqt->jqtc/dot_general | solution.py:46
  323.7 0.1 fusion.24
  323.9 0.5 fusion.2
  324.4 0.6 multiply_bitcast_fusion
  325.0 1.3 copy.25
  326.3 2.0 reshape.181
  328.3 0.0 all-reduce.2.cloned.1.call-update
  328.4 188.2 %all-reduce.2.cloned.1.call-done = f32[16560,32]{0,1:T(8,128)} async-done(((f32[16560,32]{0,1:T(8,128)}), f32[16560,32]{0,1:T(8,128)}) %all-reduce.2.cloned.1.call-update) | async-done | bytes 2119696 | tf_op jit(solution)/shard_map/psum | solution.py:66
  516.6 1.8 convolution_multiply_fusion
  (8 shorter events, 0.2 us)
Async XLA Ops:
  6.5 6.3 %copy-start.2 = (s32[16]{0:T(128)S(1)}, s32[16]{0:T(128)}, u32[]{:S(2)}) copy-start(s32[16]{0:T(128)} %param.10) | copy-start | bytes 196
  6.5 5.3 %copy-start = (f32[45,45,16]{1,2,0:T(8,128)S(1)}, f32[45,45,16]{1,2,0:T(8,128)}, u32[]{:S(2)}) copy-start(f32[45,45,16]{1,2,0:T(8,128)} %param.8) | copy-start | bytes 388804
  6.5 6.3 %copy-start.1 = (f32[45,45,16]{1,2,0:T(8,128)S(1)}, f32[45,45,16]{1,2,0:T(8,128)}, u32[]{:S(2)}) copy-start(f32[45,45,16]{1,2,0:T(8,128)} %param.7) | copy-start | bytes 388804
  6.5 280.9 %all-gather.2.cloned.1.call-start = ((), (), s32[]{:S(2)}) async-start(), calls=%async_computation | async-start | bytes 24330240 | tf_op jit(solution)/shard_map/all_gather | solution.py:44
  15.1 501.5 %all-reduce.2.cloned.1.call-start = ((), (), s32[]{:S(2)}) async-start(), calls=%async_computation.1 | async-start | bytes 4259840 | tf_op jit(solution)/shard_map/psum | solution.py:66
  19.3 4.0 copy-start.3
Sparse Core Ops, SparseCore 0:
  15.2 272.1 all-gather.1
  328.5 188.0 all-reduce.1
where the time goes:
time: 526 us; the launch traced here: 525 us
  waiting for transfers between devices  451 us (86%)
  local copies, waits for them, and re-layouts  30.4 us (6%)
  matrix products  28.3 us (5%)
  between operations  13.6 us (3%)
    all_gather x1, waiting for transfers between devices, body(): piece = lax.all_gather(fluxes, 'lon', axis=1, tiled=True)  263 us
    psum x1, waiting for transfers between devices, body(): summed = lax.psum(flat_terms, 'lat')  188 us
    dot_general x1, matrix products, body(): jnp.einsum('jic,iqt->jqtc', piece, table, precision=lax.Precision.HIGHEST)  18.9 us
    all_gather x1, local copies, waits for them, and re-layouts, body(): piece = lax.all_gather(fluxes, 'lon', axis=1, tiled=True)  17.4 us
  transfers between devices with their start and end apart: 2, of which 2 were waited for; matrix products, arithmetic and copies ran while one was open for 2% of the time, Pallas kernels for 0%

commit v1 on v0

--- a/solution.py
+++ b/solution.py
@@ -41,7 +41,9 @@
     cosine = jnp.cos(latitude)[:, None, None]
     fluxes = jnp.concatenate([eddy_u * eddy_z * cosine, eddy_v * eddy_z * cosine], axis=2)
     owned_count = slot_wavenumber.shape[0]
-    piece = lax.all_gather(fluxes, "lon", axis=1, tiled=True)
+    piece = jnp.concatenate(
+        lax.all_to_all(jnp.stack([fluxes] * lax.axis_size("lon")), "lon", 0, 0), axis=1
+    )
     table = fourier_table(slot_wavenumber, piece.shape[1])
     coeffs = jnp.einsum("jic,iqt->jqtc", piece, table, precision=lax.Precision.HIGHEST)
     present = slot_wavenumber >= 0

time: 526 us -> 662 us (1.26)
  local copies, waits for them, and re-layouts: 30.4 us -> 163 us
  waiting for transfers between devices: 451 us -> 414 us
  other arithmetic: 1.8 us -> 28.1 us
  starting transfers between devices: 0.22 us -> 13.9 us
    all_gather x1 -> x0, waiting for transfers between devices: 263 us -> none  [body(): piece = lax.all_gather(fluxes, 'lon', axis=1, tiled=True)]
    all_to_all x0 -> x1, waiting for transfers between devices: none -> 205 us  [body(): lax.all_to_all(jnp.stack([fluxes] * lax.axis_size('lon')), 'lon', 0, 0)]
    unnamed x8 -> x13, local copies, waits for them, and re-layouts: 0.02 us -> 93.2 us
    reshape x0 -> x3, local copies, waits for them, and re-layouts: none -> 59.2 us  [body(): jnp.concatenate(lax.all_to_all(jnp.stack([fluxes] * lax.axis_size('lon'))...]
    all_to_all x0 -> x1, other arithmetic: none -> 26.3 us  [body(): lax.all_to_all(jnp.stack([fluxes] * lax.axis_size('lon')), 'lon', 0, 0)]
    psum x1, waiting for transfers between devices: 188 us -> 209 us  [body(): summed = lax.psum(flat_terms, 'lat')]
    all_gather x1 -> x0, local copies, waits for them, and re-layouts: 17.4 us -> none  [body(): piece = lax.all_gather(fluxes, 'lon', axis=1, tiled=True)]
    all_to_all x0 -> x1, starting transfers between devices: none -> 13.7 us  [body(): lax.all_to_all(jnp.stack([fluxes] * lax.axis_size('lon')), 'lon', 0, 0)]
  transfers between devices with their start and end apart: 2 -> 2, of which waited for: 2 -> 2; matrix products, arithmetic and copies ran while one was open for 2% -> 1% of each run, Pallas kernels for 0% -> 0%
where the time goes in v1:
time: 662 us; the launch traced here: 661 us
  waiting for transfers between devices  414 us (63%)
  local copies, waits for them, and re-layouts  163 us (25%)
  other arithmetic  28.1 us (4%)
  matrix products  28.1 us (4%)
  starting transfers between devices  13.9 us (2%)
  between operations  13.6 us (2%)
    psum x1, waiting for transfers between devices, body(): summed = lax.psum(flat_terms, 'lat')  209 us
    all_to_all x1, waiting for transfers between devices, body(): lax.all_to_all(jnp.stack([fluxes] * lax.axis_size('lon')), 'lon', 0, 0)  205 us
    unnamed x13, local copies, waits for them, and re-layouts  93.2 us
    reshape x3, local copies, waits for them, and re-layouts, body(): jnp.concatenate(lax.all_to_all(jnp.stack([fluxes] * lax.axis_size('lon'))...  59.2 us
    all_to_all x1, other arithmetic, body(): lax.all_to_all(jnp.stack([fluxes] * lax.axis_size('lon')), 'lon', 0, 0)  26.3 us
    dot_general x1, matrix products, body(): jnp.einsum('jic,iqt->jqtc', piece, table, precision=lax.Precision.HIGHEST)  18.6 us
    all_to_all x1, starting transfers between devices, body(): lax.all_to_all(jnp.stack([fluxes] * lax.axis_size('lon')), 'lon', 0, 0)  13.7 us
  transfers between devices with their start and end apart: 2, of which 2 were waited for; matrix products, arithmetic and copies ran while one was open for 1% of the time, Pallas kernels for 0%

profile of v1, /device:TPU:1, one launch (start us, length us, event | category | flops | bytes accessed | tf_op | source)
XLA Modules:
  0.0 660.6 jit_solution(3371074014837616427)
XLA Ops:
  6.5 0.0 copy-start.3
  6.5 0.0 copy-start.1
  6.5 0.0 copy-start.2
  6.6 1.3 fusion.11
  7.9 1.4 convolution_subtract_fusion.1
  9.3 1.2 fusion.10
  10.5 1.2 fusion.12
  11.8 0.0 copy-done.1
  11.8 1.1 fusion.8
  12.9 0.0 copy-done.3
  12.9 0.0 copy-done.2
  12.9 0.4 fusion.9
  13.3 0.1 pad_maximum_fusion
  13.4 10.9 %broadcast_bitcast_fusion = f32[32,45,32,45]{3,2,1,0:T(8,128)} fusion(f32[45,45,32]{1,2,0:T(8,128)S(1)} %pad_maximum_fusion), kind=kLoop, calls=%fused_computation.76 | loop fusion | bytes 8553600
  24.2 34.5 %reshape.197 = f32[32,1,64800]{2,1,0:T(1,128)} reshape(f32[32,45,32,45]{3,2,1,0:T(8,128)} %broadcast_bitcast_fusion) | data formatting | bytes 16588800
  58.8 0.0 copy-start
  58.8 13.7 %all-to-all-start = ((f32[32,1,64800]{2,1,0:T(1,128)}), f32[32,1,64800]{2,1,0:T(1,128)}, u32[]{:S(2)}, u32[]{:S(2)}) async-start(f32[32,1,64800]{2,1,0:T(1,128)} %reshape.197), calls=%async_computation | async-start | bytes 16613376 | tf_op jit(solution)/shard_map/all_to_all | solution.py:45
  72.5 0.2 all-reduce.2.cloned.1.call-start
  72.7 0.0 copy-done
  72.7 2.9 reshape.190
  75.6 0.0 copy-start.4
  75.6 4.0 reshape.189
  79.6 0.0 copy-done.4
  79.7 0.1 fusion.32
  79.8 1.4 cosine_multiply_fusion
  81.1 204.7 %all-to-all-done = f32[32,1,64800]{2,1,0:T(1,128)} async-done(((f32[32,1,64800]{2,1,0:T(1,128)}), f32[32,1,64800]{2,1,0:T(1,128)}, u32[]{:S(2)}, u32[]{:S(2)}) %all-to-all-start) | async-done | bytes 8294432 | tf_op jit(solution)/shard_map/all_to_all | solution.py:45
  285.8 0.5 broadcast.216
  286.3 26.3 %reduce = f32[32,64800]{1,0:T(8,128)} reduce(f32[32,1,64800]{2,1,0:T(1,128)} %all-to-all-done, f32[]{:T(128)} %broadcast.216), dimensions={1}, to_apply=%all_to_all.3.reduce_sub_computation | reduce | bytes 16588804 | tf_op jit(solution)/shard_map/all_to_all | solution.py:45
  312.6 47.8 %reshape.198 = f32[32,45,32,45]{3,2,1,0:T(8,128)} reshape(f32[32,64800]{1,0:T(8,128)} %reduce) | data formatting | bytes 16588800
  360.4 9.4 %bitcast_bitcast_fusion = f32[45,32,45,32]{2,3,0,1:T(8,128)S(1)} fusion(f32[32,45,32,45]{3,2,1,0:T(8,128)} %reshape.198), kind=kLoop, calls=%fused_computation.75 | loop fusion | bytes 16588800 | tf_op jit(solution)/shard_map/reshape | solution.py:44
  369.8 28.3 %copy.27 = f32[45,32,45,32]{2,1,0,3:T(8,128)} copy(f32[45,32,45,32]{2,3,0,1:T(8,128)S(1)} %bitcast_bitcast_fusion) | data formatting | bytes 16588800 | tf_op jit(solution)/shard_map/reshape | solution.py:44
  398.1 21.5 %reshape.194 = f32[45,1440,32,1]{1,0,2,3:T(8,128)} reshape(f32[45,32,45,32]{2,1,0,3:T(8,128)} %copy.27) | data formatting | bytes 16588800 | tf_op jit(solution)/shard_map/reshape | solution.py:44
  419.6 18.6 %convolution_bitcast_fusion = f32[45,23,2,32]{0,1,3,2:T(8,128)S(1)} fusion(f32[45,1440,32,1]{1,0,2,3:T(8,128)} %reshape.194, f32[1440,23,1]{0,1,2:T(8,128)} %get-tuple-element.8, f32[1440,23,1]{0,1,2:T(8,128)S(1)} %get-tuple-element.7), kind=kOutput, calls=%fused_computation.6 | convolution fusion | flops 1144693504 | bytes 8824320 | tf_op jit(solution)/shard_map/jic,iqt->jqtc/dot_general | solution.py:48
  438.3 0.1 fusion.19
  438.5 0.5 fusion
  439.0 0.6 multiply_bitcast_fusion
  439.6 1.3 copy.25
  441.0 2.0 reshape.191
  443.0 0.0 all-reduce.2.cloned.1.call-update
  443.0 209.0 %all-reduce.2.cloned.1.call-done = f32[16560,32]{0,1:T(8,128)} async-done(((f32[16560,32]{0,1:T(8,128)}), f32[16560,32]{0,1:T(8,128)}) %all-reduce.2.cloned.1.call-update) | async-done | bytes 2119696 | tf_op jit(solution)/shard_map/psum | solution.py:68
  652.0 1.8 convolution_multiply_fusion
  (8 shorter events, 0.2 us)
Async XLA Ops:
  6.5 6.3 copy-start.3
  6.5 5.3 copy-start.1
  6.5 6.3 copy-start.2
  58.8 13.9 %copy-start = (bf16[45,16560]{1,0:T(8,128)(2,1)S(1)}, bf16[45,16560]{1,0:T(8,128)(2,1)}, u32[]{:S(2)}) copy-start(bf16[45,16560]{1,0:T(8,128)(2,1)} %param.13) | copy-start | bytes 4471204
  58.8 227.0 %all-to-all-start = ((f32[32,1,64800]{2,1,0:T(1,128)}), f32[32,1,64800]{2,1,0:T(1,128)}, u32[]{:S(2)}, u32[]{:S(2)}) async-start(f32[32,1,64800]{2,1,0:T(1,128)} %reshape.197), calls=%async_computation | async-start | bytes 16613376 | tf_op jit(solution)/shard_map/all_to_all | solution.py:45
  72.5 579.5 %all-reduce.2.cloned.1.call-start = ((), (), s32[]{:S(2)}) async-start(), calls=%async_computation.1 | async-start | bytes 4259840 | tf_op jit(solution)/shard_map/psum | solution.py:68
  75.6 4.0 copy-start.4
Sparse Core Ops, SparseCore 0:
  443.1 208.8 all-reduce.1
